TPU v7x, 32 devices: a whole 2x2x4 slice. The times are simulated.
32 devices in a mesh: groups: 2 (over y), tensor: 4 (over z), section: 4 (over x, core).
Axes of the slice: x: 2, y: 2, z: 4, core: 2. Of those that a mesh axis runs over, the one named last changes fastest.
Arguments:
- inputs: bfloat16 [4, 64, 8192], P('groups', None, 'tensor'), parts along dimension 0, may hold values from -6 to 6
- gains: bfloat16 [4, 8192], P('section'), may hold values from 0.099609375 to 1.8984375
- keep_mask: int32 [4, 128, 128], P('section', 'tensor'), may hold values from 0 to 1, as said below
- block_values: bfloat16 [4, 12288, 4096], P('section', 'tensor'), may hold values from -0.09375 to 0.09375
- head: bfloat16 [32000, 8192], P(('tensor', 'section')), may hold values from -30 to 30
- targets: int32 [4, 64], P('groups'), parts along dimension 0, may hold values from 0 to 31999
Outputs:
- token_loss: float32 [4, 64], P('groups'), parts along dimension 0
- mean_loss: float32 [2], P('groups'), parts along dimension 0
There are 2 independent parts, one for each index of `groups`. A program takes and returns all parts, laid end to end along the dimension named above; an argument that names none is the same for every part. Nothing has to cross between parts.
Inputs may be any that keep to these rules, and one draw needn't show every extreme that they name: `keep_mask`: in each section, band t (block rows t * 32 to (t + 1) * 32 - 1) keeps between 1024 and 3072 blocks, and some band of each section keeps exactly 3072. List slots past a band's count of kept blocks are not read.
All inputs are finite; a program needn't handle non-finite values.
Results may differ from a plain program's by a relative error of at most 0.0044.
The roundings to bfloat16 on the way count: a program that leaves them out, or rounds other values in their place, can miss the bound.
Values may be sent and summed in bfloat16 or wider, within the bound.
A program may use at most 320 MiB of HBM per device.

v0:
```python
import jax
import jax.numpy as jnp
from jax import lax
from jax.sharding import PartitionSpec as P

D = 8192
BLK = 64
epsilon = 1e-05


def shifted(block, axis, distance):
    devices = range(lax.axis_size(axis))
    route = [(i - distance, i) for i in devices if i - distance in devices]
    return lax.ppermute(block, axis, route)


def from_root(block, axis, source):
    block = jnp.where(lax.axis_index(axis) == source, block, jnp.zeros_like(block))
    return lax.psum(block, axis)


def joined(value, axis, combine):
    everything = jax.tree.map(lambda part: lax.all_gather(part, axis), value)
    leading = jax.tree.map(lambda part: part[0], everything)

    def turn(k, so_far):
        return combine(so_far, jax.tree.map(lambda part: part[k], everything))

    return lax.fori_loop(1, lax.axis_size(axis), turn, leading)


def merge_parts(earlier, later):
    top = jnp.maximum(earlier[0], later[0])
    total = earlier[1] * jnp.exp(earlier[0] - top) + later[1] * jnp.exp(later[0] - top)
    return (top, total, earlier[2] + later[2])


def on_device(inputs, gains, keep_mask, block_values, head, targets):
    section_count = lax.axis_size("section")
    tensor_index = lax.axis_index("tensor")
    section_index = lax.axis_index("section")
    micro_count, row_count, local_width = inputs.shape
    band_rows, block_count = (keep_mask.shape[1], keep_mask.shape[2])
    flat_mask = keep_mask[0].reshape(-1)
    slots = jnp.clip(jnp.cumsum(flat_mask, dtype=jnp.int32) - 1, 0, block_values.shape[1] - 1)
    picked = block_values[0][slots] * flat_mask[:, None].astype(jnp.bfloat16)
    panel = (
        picked.reshape(band_rows, block_count, BLK, BLK)
        .transpose(0, 2, 1, 3)
        .reshape(band_rows * BLK, D)
    )
    gain_row = gains[0]
    column_panel = lax.all_to_all(panel, "tensor", split_axis=1, concat_axis=0, tiled=True)
    timesteps = micro_count + section_count - 1
    incoming = jnp.zeros((row_count, local_width), jnp.bfloat16)
    finished = [None] * micro_count
    for moment in range(timesteps):
        current = jnp.where(section_index == 0, inputs[min(moment, micro_count - 1)], incoming)
        apply_widened = lax.all_gather(current, "tensor", axis=1, tiled=True).astype(jnp.float32)
        scaled = (apply_widened * gain_row.astype(jnp.float32)).astype(jnp.bfloat16)
        projected = jnp.dot(scaled, column_panel, preferred_element_type=jnp.float32)
        projected, apply_sumsq = (projected, jnp.sum(apply_widened * apply_widened, axis=1))
        update = projected * lax.rsqrt(apply_sumsq[:, None] / D + epsilon)
        outgoing = (current.astype(jnp.float32) + update).astype(jnp.bfloat16)
        done_index = moment - (section_count - 1)
        if 0 <= done_index < micro_count:
            finished[done_index] = outgoing
        if moment < timesteps - 1:
            incoming = shifted(outgoing, "section", 1)
    final_rows = jnp.stack(finished).reshape(micro_count * row_count, local_width)
    vocab_rows = head.shape[0]
    relayed = from_root(final_rows, "section", section_count - 1)
    portion = lax.all_gather(relayed, "tensor", axis=1, tiled=True)
    raw_logits = lax.dot_general(
        portion, head, (((1,), (1,)), ((), ())), preferred_element_type=jnp.float32
    )
    widened = portion.astype(jnp.float32)
    raw_logits, final_sumsq = (raw_logits, jnp.sum(widened * widened, axis=1))
    logits = raw_logits * lax.rsqrt(final_sumsq[:, None] / D + epsilon)
    vocab_start = (tensor_index * section_count + section_index) * vocab_rows
    local_ids = targets.reshape(-1) - vocab_start
    matches = jnp.arange(vocab_rows, dtype=jnp.int32)[None, :] == local_ids[:, None]
    target_logit = jnp.sum(jnp.where(matches, logits, 0.0), axis=1)
    local_top = jnp.max(logits, axis=1)
    local_total = jnp.sum(jnp.exp(logits - local_top[:, None]), axis=1)
    top, total, chosen = joined(
        (local_top, local_total, target_logit), ("tensor", "section"), merge_parts
    )
    token_loss = (top + jnp.log(total) - chosen).reshape(micro_count, row_count)
    mean_loss = jnp.mean(token_loss).reshape(1)
    return (token_loss, mean_loss)


def solution(mesh):
    placed = (
        P("groups", None, "tensor"),
        P("section", None),
        P("section", "tensor", None),
        P("section", "tensor", None),
        P(("tensor", "section"), None),
        P("groups", None),
    )
    return jax.shard_map(
        on_device,
        mesh=mesh,
        in_specs=placed,
        out_specs=(P("groups", None), P("groups")),
        check_vma=False,
    )
```

profile of v0, /device:TPU:0, one launch (start us, length us, event | category | flops | bytes accessed | tf_op | source)
XLA Modules:
  0.0 1553.3 jit_solution(10972753995354582155)
XLA Ops:
  9.3 67.2 %gather_fusion = bf16[4096,4096]{1,0:T(8,128)(2,1)} fusion(bf16[3072,4096]{1,0:T(8,128)(2,1)} %bitcast.77, s32[4096]{0:T(1024)S(1)} %broadcast_clamp_fusion), kind=kCustom, calls=%fused_computation | custom fusion | bytes 67125248 | tf_op jit(solution)/shard_map/gather | solution.py:46
  76.4 41.0 %copy.11 = bf16[4096,4096]{0,1:T(8,128)(2,1)} copy(bf16[4096,4096]{1,0:T(8,128)(2,1)} %gather_fusion) | data formatting | bytes 67108864 | tf_op jit(solution)/shard_map/gather | solution.py:46
  117.4 23.1 %copy.14 = bf16[512,8,32,128]{3,2,1,0:T(8,128)(2,1)} copy(bf16[512,8,32,128]{3,1,2,0:T(8,128)(2,1)} %bitcast.84) | data formatting | bytes 67108864
  140.5 23.1 %multiply_bitcast_fusion = bf16[32,64,128,64]{2,0,3,1:T(8,128)(2,1)} fusion(bf16[32,128,64,64]{1,0,3,2:T(8,128)(2,1)} %bitcast.83, bf16[32,128]{1,0:T(8,128)(2,1)S(1)} %bitcast_convert_fusion), kind=kLoop, calls=%fused_computation.11 | loop fusion | flops 16777216 | bytes 67117056 | tf_op jit(solution)/shard_map/transpose | solution.py:49
  163.6 110.4 %copy.12 = bf16[32,64,128,64]{1,0,3,2:T(8,128)(2,1)} copy(bf16[32,64,128,64]{2,0,3,1:T(8,128)(2,1)} %multiply_bitcast_fusion) | data formatting | bytes 67108864 | tf_op jit(solution)/shard_map/transpose | solution.py:49
  274.0 90.3 %all_to_all.14 = bf16[2048,4,2048]{0,2,1:T(8,128)(2,1)} reshape(bf16[32,64,128,64]{1,0,3,2:T(8,128)(2,1)} %copy.12) | data formatting | bytes 67108864 | tf_op jit(solution)/shard_map/all_to_all | solution.py:53
  375.6 210.2 %all-gather.24.cloned.1.call-done = bf16[1,64,8192]{2,1,0:T(8,128)(2,1)} async-done(((bf16[1,64,2048]{2,1,0:T(8,128)(2,1)}), bf16[1,64,8192]{2,1,0:T(8,128)(2,1)}) %all-gather.24.cloned.1.call-update) | async-done | bytes 1048592 | tf_op jit(solution)/shard_map/all_gather | solution.py:59
  587.4 527.8 %all-to-all-done = bf16[2048,4,2048]{0,2,1:T(8,128)(2,1)} async-done(((bf16[2048,4,2048]{0,2,1:T(8,128)(2,1)}), bf16[2048,4,2048]{0,2,1:T(8,128)(2,1)}, u32[]{:S(2)}, u32[]{:S(2)}) %all-to-all-start) | async-done | bytes 33554464 | tf_op jit(solution)/shard_map/all_to_all | solution.py:53
  1115.1 42.8 %copy.13 = bf16[4,2048,2048]{2,1,0:T(8,128)(2,1)} copy(bf16[4,2048,2048]{1,2,0:T(8,128)(2,1)} %bitcast.12) | data formatting | bytes 67108864 | tf_op jit(solution)/shard_map/all_to_all | solution.py:53
  1157.9 13.7 fusion.8
  1174.9 32.4 %all-gather.14.cloned.1.call-done = bf16[64,8192]{1,0:T(8,128)(2,1)} async-done(((bf16[64,2048]{1,0:T(8,128)(2,1)}), bf16[64,8192]{1,0:T(8,128)(2,1)}) %all-gather.14.cloned.1.call-update) | async-done | bytes 1048592 | tf_op jit(solution)/shard_map/all_gather | solution.py:59
  1208.9 16.8 %add_convert_fusion.3 = bf16[64,2048]{1,0:T(8,128)(2,1)S(1)} fusion(bf16[64,2048]{1,0:T(8,128)(2,1)} %bitcast_select_fusion.3, f32[64]{0:T(128)S(1)} %add_rsqrt_fusion.4, bf16[8192,2048]{1,0:T(8,128)(2,1)} %bitcast.79, bf16[64,8192]{1,0:T(8,128)(2,1)} %all-gather.14.cloned.1.call-done, f32[8192]{0:T(1024)S(1)} %bitcast.86), kind=kOutput, calls=%fused_computation.54 | convolution fusion | flops 2149580800 | bytes 35160320 | tf_op jit(solution)/shard_map/dot_general | solution.py:61
  1229.4 32.3 %all-gather.16.cloned.1.call-done = bf16[64,8192]{1,0:T(8,128)(2,1)} async-done(((bf16[64,2048]{1,0:T(8,128)(2,1)}), bf16[64,8192]{1,0:T(8,128)(2,1)}) %all-gather.16.cloned.1.call-update) | async-done | bytes 1048592 | tf_op jit(solution)/shard_map/all_gather | solution.py:59
  1263.2 16.8 %add_convert_fusion.2 = bf16[64,2048]{1,0:T(8,128)(2,1)S(1)} fusion(bf16[64,2048]{1,0:T(8,128)(2,1)} %bitcast_select_fusion.2, f32[64]{0:T(128)S(1)} %add_rsqrt_fusion.3, bf16[8192,2048]{1,0:T(8,128)(2,1)} %bitcast.80, bf16[64,8192]{1,0:T(8,128)(2,1)} %all-gather.16.cloned.1.call-done, f32[8192]{0:T(1024)S(1)} %bitcast.87), kind=kOutput, calls=%fused_computation.53 | convolution fusion | flops 2149580800 | bytes 35160320 | tf_op jit(solution)/shard_map/dot_general | solution.py:61
  1283.6 32.5 %all-gather.18.cloned.1.call-done = bf16[64,8192]{1,0:T(8,128)(2,1)} async-done(((bf16[64,2048]{1,0:T(8,128)(2,1)}), bf16[64,8192]{1,0:T(8,128)(2,1)}) %all-gather.18.cloned.1.call-update) | async-done | bytes 1048592 | tf_op jit(solution)/shard_map/all_gather | solution.py:59
  1317.6 16.8 %add_convert_fusion.1 = bf16[64,2048]{1,0:T(8,128)(2,1)S(1)} fusion(bf16[64,2048]{1,0:T(8,128)(2,1)} %bitcast_select_fusion.1, f32[64]{0:T(128)S(1)} %add_rsqrt_fusion.2, bf16[8192,2048]{1,0:T(8,128)(2,1)} %bitcast.81, bf16[64,8192]{1,0:T(8,128)(2,1)} %all-gather.18.cloned.1.call-done, f32[8192]{0:T(1024)S(1)} %bitcast.88), kind=kOutput, calls=%fused_computation.52 | convolution fusion | flops 2149580800 | bytes 35160320 | tf_op jit(solution)/shard_map/dot_general | solution.py:61
  1338.2 32.3 %all-gather.20.cloned.1.call-done = bf16[64,8192]{1,0:T(8,128)(2,1)} async-done(((bf16[64,2048]{1,0:T(8,128)(2,1)}), bf16[64,8192]{1,0:T(8,128)(2,1)}) %all-gather.20.cloned.1.call-update) | async-done | bytes 1048592 | tf_op jit(solution)/shard_map/all_gather | solution.py:59
  1372.0 16.8 %fusion.30 = bf16[1,64,2048]{2,1,0:T(8,128)(2,1)S(1)} fusion(bf16[64,2048]{1,0:T(8,128)(2,1)} %bitcast_select_fusion, f32[64]{0:T(128)S(1)} %add_rsqrt_fusion.1, bf16[8192,2048]{1,0:T(8,128)(2,1)} %bitcast.82, bf16[64,8192]{1,0:T(8,128)(2,1)} %all-gather.20.cloned.1.call-done, f32[8192]{0:T(1024)S(1)} %bitcast.89), kind=kOutput, calls=%fused_computation.55 | convolution fusion | flops 2149580800 | bytes 35160320 | tf_op jit(solution)/shard_map/dot_general | solution.py:61
  1389.7 32.8 %all-reduce.2.cloned.1.call-done = bf16[128,2048]{1,0:T(8,128)(2,1)} async-done(((bf16[128,2048]{1,0:T(8,128)(2,1)}), bf16[128,2048]{1,0:T(8,128)(2,1)}) %all-reduce.2.cloned.1.call-update) | async-done | bytes 524304 | tf_op jit(solution)/shard_map/psum | solution.py:19
  1422.7 47.4 %all-gather.22.cloned.1.call-done = bf16[128,8192]{1,0:T(8,128)(2,1)} async-done(((bf16[128,2048]{1,0:T(8,128)(2,1)}), bf16[128,8192]{1,0:T(8,128)(2,1)}) %all-gather.22.cloned.1.call-update) | async-done | bytes 2097168 | tf_op jit(solution)/shard_map/all_gather | solution.py:73
  1472.2 15.0 fusion.41
  1487.3 19.0 %all-gather.4 = f32[16,1,128]{2,1,0:T(1,128)S(1)} all-gather(f32[1,1,128]{2,1,0:T(1,128)S(1)} %bitcast.98), channel_id=3, replica_groups=mesh['groups'=2,'tensor'=4,'section'=4] {'tensor','section'}, dimensions={0}, use_global_device_ids=true | all-gather | bytes 8704 | tf_op jit(solution)/shard_map/all_gather | solution.py:23
  1506.6 17.3 %all-gather.5 = f32[16,1,128]{2,1,0:T(1,128)S(1)} all-gather(f32[1,1,128]{2,1,0:T(1,128)S(1)} %bitcast.100), channel_id=4, replica_groups=mesh['groups'=2,'tensor'=4,'section'=4] {'tensor','section'}, dimensions={0}, use_global_device_ids=true | all-gather | bytes 8704 | tf_op jit(solution)/shard_map/all_gather | solution.py:23
  1523.9 18.7 %all-gather.6 = f32[16,1,128]{2,1,0:T(1,128)S(1)} all-gather(f32[1,1,128]{2,1,0:T(1,128)S(1)} %bitcast.99), channel_id=5, replica_groups=mesh['groups'=2,'tensor'=4,'section'=4] {'tensor','section'}, dimensions={0}, use_global_device_ids=true | all-gather | bytes 8704 | tf_op jit(solution)/shard_map/all_gather | solution.py:23
  (84 shorter events, 40.9 us)
Async XLA Ops:
  364.3 9.9 copy-start.1
  364.3 11.2 copy-start.3
  364.4 750.8 %all-to-all-start = ((bf16[2048,4,2048]{0,2,1:T(8,128)(2,1)}), bf16[2048,4,2048]{0,2,1:T(8,128)(2,1)}, u32[]{:S(2)}, u32[]{:S(2)}) async-start(bf16[2048,4,2048]{0,2,1:T(8,128)(2,1)} %all_to_all.14), calls=%async_computation | async-start | bytes 67108864 | tf_op jit(solution)/shard_map/all_to_all | solution.py:53
  374.2 211.6 %all-gather.24.cloned.1.call-start = ((), (), s32[]{:S(2)}) async-start(), calls=%async_computation.7 | async-start | bytes 1310720 | tf_op jit(solution)/shard_map/all_gather | solution.py:59
  375.0 832.3 %all-gather.14.cloned.1.call-start = ((), (), s32[]{:S(2)}) async-start(), calls=%async_computation.1 | async-start | bytes 1310720 | tf_op jit(solution)/shard_map/all_gather | solution.py:59
  1115.1 42.8 %copy-start = (bf16[1,64,8192]{2,1,0:T(8,128)(2,1)S(1)}, bf16[1,64,8192]{2,1,0:T(8,128)(2,1)}, u32[]{:S(2)}) copy-start(bf16[1,64,8192]{2,1,0:T(8,128)(2,1)} %all-gather.24.cloned.1.call-done) | copy-start | bytes 3145732
  1115.1 42.8 %copy-start.2 = (bf16[1,64,2048]{2,1,0:T(8,128)(2,1)S(1)}, bf16[1,64,2048]{2,1,0:T(8,128)(2,1)}, u32[]{:S(2)}) copy-start(bf16[1,64,2048]{2,1,0:T(8,128)(2,1)} %slice_select_fusion) | copy-start | bytes 786436
  1171.7 2.4 collective-permute-start
  1174.8 86.8 %all-gather.16.cloned.1.call-start = ((), (), s32[]{:S(2)}) async-start(), calls=%async_computation.2 | async-start | bytes 1310720 | tf_op jit(solution)/shard_map/all_gather | solution.py:59
  1225.7 2.8 collective-permute-start.1
  1229.2 86.9 %all-gather.18.cloned.1.call-start = ((), (), s32[]{:S(2)}) async-start(), calls=%async_computation.3 | async-start | bytes 1310720 | tf_op jit(solution)/shard_map/all_gather | solution.py:59
  1280.0 2.8 collective-permute-start.2
  1283.5 86.9 %all-gather.20.cloned.1.call-start = ((), (), s32[]{:S(2)}) async-start(), calls=%async_computation.4 | async-start | bytes 1310720 | tf_op jit(solution)/shard_map/all_gather | solution.py:59
  1334.4 88.2 %copy-start.4 = (s32[2,64]{1,0:T(2,128)S(1)}, s32[2,64]{1,0:T(2,128)}, u32[]{:S(2)}) copy-start(s32[2,64]{1,0:T(2,128)} %param.13) | copy-start | bytes 1540
  1334.4 2.8 collective-permute-start.3
  1337.9 84.6 %all-reduce.2.cloned.1.call-start = ((), (), s32[]{:S(2)}) async-start(), calls=%async_computation.5 | async-start | bytes 1048576 | tf_op jit(solution)/shard_map/psum | solution.py:19
  1389.7 80.4 %all-gather.22.cloned.1.call-start = ((), (), s32[]{:S(2)}) async-start(), calls=%async_computation.6 | async-start | bytes 2621440 | tf_op jit(solution)/shard_map/all_gather | solution.py:73
Sparse Core Ops, SparseCore 0:
  376.6 209.1 all-gather.23
  1175.0 32.3 all-gather.13
  1229.3 32.3 all-gather.15
  1283.7 32.3 all-gather.17
  1338.0 32.3 all-gather.19
  1389.8 32.7 all-reduce.1
  1424.1 45.9 all-gather.21
where the time goes:
time: 1570 us; the launch traced here: 1550 us
  waiting for transfers between devices  952 us (61%)
  local copies, waits for them, and re-layouts  376 us (24%)
  matrix products  95.9 us (6%)
  blocking collectives  55 us (4%)
  other arithmetic  40.6 us (3%)
  starting transfers between devices  17.1 us (1%)
  between operations  16.4 us (1%)
    all_to_all x1, waiting for transfers between devices, on_device(): lax.all_to_all(panel, 'tensor', split_axis=1, concat_axis=0, tiled=True)  528 us
    all_gather x5, waiting for transfers between devices, on_device(): lax.all_gather(current, 'tensor', axis=1, tiled=True).astype(jnp.float32)  340 us
    all_to_all x2, local copies, waits for them, and re-layouts, on_device(): lax.all_to_all(panel, 'tensor', split_axis=1, concat_axis=0, tiled=True)  133 us
    transpose x1, local copies, waits for them, and re-layouts, on_device(): panel = picked.reshape(band_rows, block_count, BLK, BLK).transpose(0, 2,...  110 us
    gather x2, local copies, waits for them, and re-layouts, on_device(): picked = block_values[0][slots] * flat_mask[:, None].astype(jnp.bfloat16)  108 us
    dot_general x5, matrix products, on_device(): jnp.dot(scaled, column_panel, preferred_element_type=jnp.float32)  80.9 us
    all_gather x3, blocking collectives, joined(): everything = jax.tree.map(lambda part: lax.all_gather(part, axis), value)  55 us
    all_gather x1, waiting for transfers between devices, on_device(): portion = lax.all_gather(relayed, 'tensor', axis=1, tiled=True)  47.4 us
  transfers between devices with their start and end apart: 12, of which 12 were waited for; matrix products, arithmetic and copies ran while one was open for 0% of the time, Pallas kernels for 0%

commit v1 on v0

--- a/solution.py
+++ b/solution.py
@@ -6,6 +6,19 @@
 D = 8192
 BLK = 64
 epsilon = 1e-05
+
+
+def collect(array, axis, dim):
+    ways = lax.axis_size(axis)
+    up = [(d, (d + 1) % ways) for d in range(ways)]
+    down = [(d, (d - 1) % ways) for d in range(ways)]
+    earlier, later = ([array], [array])
+    for _ in range(ways // 2):
+        earlier.append(lax.ppermute(earlier[-1], axis, up))
+    for _ in range((ways - 1) // 2):
+        later.append(lax.ppermute(later[-1], axis, down))
+    line = jnp.concatenate([*earlier[::-1], *later[1:]], axis=dim)
+    return jnp.roll(line, (lax.axis_index(axis) - ways // 2) * array.shape[dim], axis=dim)
 
 
 def shifted(block, axis, distance):
@@ -70,7 +83,7 @@
     final_rows = jnp.stack(finished).reshape(micro_count * row_count, local_width)
     vocab_rows = head.shape[0]
     relayed = from_root(final_rows, "section", section_count - 1)
-    portion = lax.all_gather(relayed, "tensor", axis=1, tiled=True)
+    portion = collect(relayed, "tensor", 1)
     raw_logits = lax.dot_general(
         portion, head, (((1,), (1,)), ((), ())), preferred_element_type=jnp.float32
     )

time: 1570 us -> 1550 us (0.987)
  waiting for transfers between devices: 952 us -> 936 us
    all_gather x1 -> x0, waiting for transfers between devices: 47.4 us -> none  [on_device(): portion = lax.all_gather(relayed, 'tensor', axis=1, tiled=True)]
    ppermute x0 -> x3, waiting for transfers between devices: none -> 31.2 us  [the longest x2 25.9 us: collect(): earlier.append(lax.ppermute(earlier[-1], axis, up))]
  transfers between devices with their start and end apart: 12 -> 14, of which waited for: 12 -> 14; matrix products, arithmetic and copies ran while one was open for 0% -> 0% of each run, Pallas kernels for 0% -> 0%
where the time goes in v1:
time: 1550 us; the launch traced here: 1540 us
  waiting for transfers between devices  936 us (60%)
  local copies, waits for them, and re-layouts  377 us (24%)
  matrix products  95.3 us (6%)
  blocking collectives  55.6 us (4%)
  other arithmetic  39 us (3%)
  starting transfers between devices  22.4 us (1%)
  between operations  16.4 us (1%)
    all_to_all x1, waiting for transfers between devices, on_device(): lax.all_to_all(panel, 'tensor', split_axis=1, concat_axis=0, tiled=True)  528 us
    all_gather x5, waiting for transfers between devices, on_device(): lax.all_gather(current, 'tensor', axis=1, tiled=True).astype(jnp.float32)  340 us
    all_to_all x2, local copies, waits for them, and re-layouts, on_device(): lax.all_to_all(panel, 'tensor', split_axis=1, concat_axis=0, tiled=True)  133 us
    transpose x1, local copies, waits for them, and re-layouts, on_device(): panel = picked.reshape(band_rows, block_count, BLK, BLK).transpose(0, 2,...  110 us
    gather x2, local copies, waits for them, and re-layouts, on_device(): picked = block_values[0][slots] * flat_mask[:, None].astype(jnp.bfloat16)  108 us
    dot_general x5, matrix products, on_device(): jnp.dot(scaled, column_panel, preferred_element_type=jnp.float32)  80.9 us
    all_gather x3, blocking collectives, joined(): everything = jax.tree.map(lambda part: lax.all_gather(part, axis), value)  55.6 us
    psum x1, waiting for transfers between devices, from_root(): return lax.psum(block, axis)  32.9 us
  transfers between devices with their start and end apart: 14, of which 14 were waited for; matrix products, arithmetic and copies ran while one was open for 0% of the time, Pallas kernels for 0%

profile of v1, /device:TPU:0, one launch (start us, length us, event | category | flops | bytes accessed | tf_op | source)
XLA Modules:
  0.0 1542.2 jit_solution(6049712685755973413)
XLA Ops:
  9.3 67.2 %gather_fusion = bf16[4096,4096]{1,0:T(8,128)(2,1)} fusion(bf16[3072,4096]{1,0:T(8,128)(2,1)} %bitcast.76, s32[4096]{0:T(1024)S(1)} %broadcast_clamp_fusion), kind=kCustom, calls=%fused_computation | custom fusion | bytes 67125248 | tf_op jit(solution)/shard_map/gather | solution.py:59
  76.4 41.0 %copy.11 = bf16[4096,4096]{0,1:T(8,128)(2,1)} copy(bf16[4096,4096]{1,0:T(8,128)(2,1)} %gather_fusion) | data formatting | bytes 67108864 | tf_op jit(solution)/shard_map/gather | solution.py:59
  117.4 23.1 %copy.14 = bf16[512,8,32,128]{3,2,1,0:T(8,128)(2,1)} copy(bf16[512,8,32,128]{3,1,2,0:T(8,128)(2,1)} %bitcast.83) | data formatting | bytes 67108864
  140.5 23.1 %multiply_bitcast_fusion = bf16[32,64,128,64]{2,0,3,1:T(8,128)(2,1)} fusion(bf16[32,128,64,64]{1,0,3,2:T(8,128)(2,1)} %bitcast.82, bf16[32,128]{1,0:T(8,128)(2,1)S(1)} %bitcast_convert_fusion), kind=kLoop, calls=%fused_computation.11 | loop fusion | flops 16777216 | bytes 67117056 | tf_op jit(solution)/shard_map/transpose | solution.py:62
  163.6 110.4 %copy.12 = bf16[32,64,128,64]{1,0,3,2:T(8,128)(2,1)} copy(bf16[32,64,128,64]{2,0,3,1:T(8,128)(2,1)} %multiply_bitcast_fusion) | data formatting | bytes 67108864 | tf_op jit(solution)/shard_map/transpose | solution.py:62
  274.0 90.3 %all_to_all.14 = bf16[2048,4,2048]{0,2,1:T(8,128)(2,1)} reshape(bf16[32,64,128,64]{1,0,3,2:T(8,128)(2,1)} %copy.12) | data formatting | bytes 67108864 | tf_op jit(solution)/shard_map/all_to_all | solution.py:66
  375.6 210.2 %all-gather.21.cloned.1.call-done = bf16[1,64,8192]{2,1,0:T(8,128)(2,1)} async-done(((bf16[1,64,2048]{2,1,0:T(8,128)(2,1)}), bf16[1,64,8192]{2,1,0:T(8,128)(2,1)}) %all-gather.21.cloned.1.call-update) | async-done | bytes 1048592 | tf_op jit(solution)/shard_map/all_gather | solution.py:72
  587.4 527.8 %all-to-all-done = bf16[2048,4,2048]{0,2,1:T(8,128)(2,1)} async-done(((bf16[2048,4,2048]{0,2,1:T(8,128)(2,1)}), bf16[2048,4,2048]{0,2,1:T(8,128)(2,1)}, u32[]{:S(2)}, u32[]{:S(2)}) %all-to-all-start) | async-done | bytes 33554464 | tf_op jit(solution)/shard_map/all_to_all | solution.py:66
  1115.1 42.8 %copy.13 = bf16[4,2048,2048]{2,1,0:T(8,128)(2,1)} copy(bf16[4,2048,2048]{1,2,0:T(8,128)(2,1)} %bitcast.12) | data formatting | bytes 67108864 | tf_op jit(solution)/shard_map/all_to_all | solution.py:66
  1157.9 13.7 fusion.8
  1174.9 32.4 %all-gather.13.cloned.1.call-done = bf16[64,8192]{1,0:T(8,128)(2,1)} async-done(((bf16[64,2048]{1,0:T(8,128)(2,1)}), bf16[64,8192]{1,0:T(8,128)(2,1)}) %all-gather.13.cloned.1.call-update) | async-done | bytes 1048592 | tf_op jit(solution)/shard_map/all_gather | solution.py:72
  1208.9 16.8 %add_convert_fusion.3 = bf16[64,2048]{1,0:T(8,128)(2,1)S(1)} fusion(bf16[64,2048]{1,0:T(8,128)(2,1)} %bitcast_select_fusion.3, f32[64]{0:T(128)S(1)} %add_rsqrt_fusion.4, bf16[8192,2048]{1,0:T(8,128)(2,1)} %bitcast.78, bf16[64,8192]{1,0:T(8,128)(2,1)} %all-gather.13.cloned.1.call-done, f32[8192]{0:T(1024)S(1)} %bitcast.85), kind=kOutput, calls=%fused_computation.55 | convolution fusion | flops 2149580800 | bytes 35160320 | tf_op jit(solution)/shard_map/dot_general | solution.py:74
  1229.4 32.3 %all-gather.15.cloned.1.call-done = bf16[64,8192]{1,0:T(8,128)(2,1)} async-done(((bf16[64,2048]{1,0:T(8,128)(2,1)}), bf16[64,8192]{1,0:T(8,128)(2,1)}) %all-gather.15.cloned.1.call-update) | async-done | bytes 1048592 | tf_op jit(solution)/shard_map/all_gather | solution.py:72
  1263.2 16.8 %add_convert_fusion.2 = bf16[64,2048]{1,0:T(8,128)(2,1)S(1)} fusion(bf16[64,2048]{1,0:T(8,128)(2,1)} %bitcast_select_fusion.2, f32[64]{0:T(128)S(1)} %add_rsqrt_fusion.3, bf16[8192,2048]{1,0:T(8,128)(2,1)} %bitcast.79, bf16[64,8192]{1,0:T(8,128)(2,1)} %all-gather.15.cloned.1.call-done, f32[8192]{0:T(1024)S(1)} %bitcast.86), kind=kOutput, calls=%fused_computation.54 | convolution fusion | flops 2149580800 | bytes 35160320 | tf_op jit(solution)/shard_map/dot_general | solution.py:74
  1283.6 32.5 %all-gather.17.cloned.1.call-done = bf16[64,8192]{1,0:T(8,128)(2,1)} async-done(((bf16[64,2048]{1,0:T(8,128)(2,1)}), bf16[64,8192]{1,0:T(8,128)(2,1)}) %all-gather.17.cloned.1.call-update) | async-done | bytes 1048592 | tf_op jit(solution)/shard_map/all_gather | solution.py:72
  1317.6 16.8 %add_convert_fusion.1 = bf16[64,2048]{1,0:T(8,128)(2,1)S(1)} fusion(bf16[64,2048]{1,0:T(8,128)(2,1)} %bitcast_select_fusion.1, f32[64]{0:T(128)S(1)} %add_rsqrt_fusion.2, bf16[8192,2048]{1,0:T(8,128)(2,1)} %bitcast.80, bf16[64,8192]{1,0:T(8,128)(2,1)} %all-gather.17.cloned.1.call-done, f32[8192]{0:T(1024)S(1)} %bitcast.87), kind=kOutput, calls=%fused_computation.53 | convolution fusion | flops 2149580800 | bytes 35160320 | tf_op jit(solution)/shard_map/dot_general | solution.py:74
  1338.2 32.3 %all-gather.19.cloned.1.call-done = bf16[64,8192]{1,0:T(8,128)(2,1)} async-done(((bf16[64,2048]{1,0:T(8,128)(2,1)}), bf16[64,8192]{1,0:T(8,128)(2,1)}) %all-gather.19.cloned.1.call-update) | async-done | bytes 1048592 | tf_op jit(solution)/shard_map/all_gather | solution.py:72
  1372.0 16.8 %fusion.31 = bf16[1,64,2048]{2,1,0:T(8,128)(2,1)S(1)} fusion(bf16[64,2048]{1,0:T(8,128)(2,1)} %bitcast_select_fusion, f32[64]{0:T(128)S(1)} %add_rsqrt_fusion.1, bf16[8192,2048]{1,0:T(8,128)(2,1)} %bitcast.81, bf16[64,8192]{1,0:T(8,128)(2,1)} %all-gather.19.cloned.1.call-done, f32[8192]{0:T(1024)S(1)} %bitcast.88), kind=kOutput, calls=%fused_computation.56 | convolution fusion | flops 2149580800 | bytes 35160320 | tf_op jit(solution)/shard_map/dot_general | solution.py:74
  1389.7 32.9 %all-reduce.2.cloned.1.call-done = bf16[128,2048]{1,0:T(8,128)(2,1)} async-done(((bf16[128,2048]{1,0:T(8,128)(2,1)}), bf16[128,2048]{1,0:T(8,128)(2,1)}) %all-reduce.2.cloned.1.call-update) | async-done | bytes 524304 | tf_op jit(solution)/shard_map/psum | solution.py:32
  1424.0 13.1 collective-permute-done.4
  1461.1 14.5 fusion.43
  1475.6 19.6 %all-gather.4 = f32[16,1,128]{2,1,0:T(1,128)S(1)} all-gather(f32[1,1,128]{2,1,0:T(1,128)S(1)} %bitcast.97), channel_id=3, replica_groups=mesh['groups'=2,'tensor'=4,'section'=4] {'tensor','section'}, dimensions={0}, use_global_device_ids=true | all-gather | bytes 8704 | tf_op jit(solution)/shard_map/all_gather | solution.py:36
  1495.5 17.3 %all-gather.5 = f32[16,1,128]{2,1,0:T(1,128)S(1)} all-gather(f32[1,1,128]{2,1,0:T(1,128)S(1)} %bitcast.99), channel_id=4, replica_groups=mesh['groups'=2,'tensor'=4,'section'=4] {'tensor','section'}, dimensions={0}, use_global_device_ids=true | all-gather | bytes 8704 | tf_op jit(solution)/shard_map/all_gather | solution.py:36
  1512.8 18.7 %all-gather.6 = f32[16,1,128]{2,1,0:T(1,128)S(1)} all-gather(f32[1,1,128]{2,1,0:T(1,128)S(1)} %bitcast.98), channel_id=5, replica_groups=mesh['groups'=2,'tensor'=4,'section'=4] {'tensor','section'}, dimensions={0}, use_global_device_ids=true | all-gather | bytes 8704 | tf_op jit(solution)/shard_map/all_gather | solution.py:36
  (97 shorter events, 64.0 us)
Async XLA Ops:
  364.3 9.9 copy-start.1
  364.3 11.2 copy-start.4
  364.4 750.8 %all-to-all-start = ((bf16[2048,4,2048]{0,2,1:T(8,128)(2,1)}), bf16[2048,4,2048]{0,2,1:T(8,128)(2,1)}, u32[]{:S(2)}, u32[]{:S(2)}) async-start(bf16[2048,4,2048]{0,2,1:T(8,128)(2,1)} %all_to_all.14), calls=%async_computation | async-start | bytes 67108864 | tf_op jit(solution)/shard_map/all_to_all | solution.py:66
  374.2 211.6 %all-gather.21.cloned.1.call-start = ((), (), s32[]{:S(2)}) async-start(), calls=%async_computation.6 | async-start | bytes 1310720 | tf_op jit(solution)/shard_map/all_gather | solution.py:72
  375.0 832.3 %all-gather.13.cloned.1.call-start = ((), (), s32[]{:S(2)}) async-start(), calls=%async_computation.1 | async-start | bytes 1310720 | tf_op jit(solution)/shard_map/all_gather | solution.py:72
  1115.1 42.8 %copy-start = (bf16[1,64,8192]{2,1,0:T(8,128)(2,1)S(1)}, bf16[1,64,8192]{2,1,0:T(8,128)(2,1)}, u32[]{:S(2)}) copy-start(bf16[1,64,8192]{2,1,0:T(8,128)(2,1)} %all-gather.21.cloned.1.call-done) | copy-start | bytes 3145732
  1115.1 42.8 %copy-start.2 = (bf16[1,64,2048]{2,1,0:T(8,128)(2,1)S(1)}, bf16[1,64,2048]{2,1,0:T(8,128)(2,1)}, u32[]{:S(2)}) copy-start(bf16[1,64,2048]{2,1,0:T(8,128)(2,1)} %slice_select_fusion) | copy-start | bytes 786436
  1171.7 2.4 collective-permute-start
  1174.8 86.8 %all-gather.15.cloned.1.call-start = ((), (), s32[]{:S(2)}) async-start(), calls=%async_computation.2 | async-start | bytes 1310720 | tf_op jit(solution)/shard_map/all_gather | solution.py:72
  1225.7 2.8 collective-permute-start.1
  1229.2 86.9 %all-gather.17.cloned.1.call-start = ((), (), s32[]{:S(2)}) async-start(), calls=%async_computation.3 | async-start | bytes 1310720 | tf_op jit(solution)/shard_map/all_gather | solution.py:72
  1280.0 2.8 collective-permute-start.2
  1283.5 86.9 %all-gather.19.cloned.1.call-start = ((), (), s32[]{:S(2)}) async-start(), calls=%async_computation.4 | async-start | bytes 1310720 | tf_op jit(solution)/shard_map/all_gather | solution.py:72
  1334.4 2.8 collective-permute-start.3
  1337.9 84.6 %all-reduce.2.cloned.1.call-start = ((), (), s32[]{:S(2)}) async-start(), calls=%async_computation.5 | async-start | bytes 1048576 | tf_op jit(solution)/shard_map/psum | solution.py:32
  1372.0 65.2 %copy-start.5 = (s32[2,64]{1,0:T(2,128)S(1)}, s32[2,64]{1,0:T(2,128)}, u32[]{:S(2)}) copy-start(s32[2,64]{1,0:T(2,128)} %param.13) | copy-start | bytes 1540
  1422.5 38.0 %copy-start.3 = (bf16[128,2048]{1,0:T(8,128)(2,1)S(1)}, bf16[128,2048]{1,0:T(8,128)(2,1)}, u32[]{:S(2)}) copy-start(bf16[128,2048]{1,0:T(8,128)(2,1)} %all-reduce.2.cloned.1.call-done) | copy-start | bytes 1572868
  1422.6 14.6 collective-permute-start.4
  1437.2 16.7 %collective-permute-start.5 = (bf16[128,2048]{1,0:T(8,128)(2,1)S(1)}, bf16[128,2048]{1,0:T(8,128)(2,1)S(1)}, u32[]{:S(2)}, u32[]{:S(2)}) collective-permute-start(bf16[128,2048]{1,0:T(8,128)(2,1)S(1)} %collective-permute-done.4), channel_id=1, source_target_pairs={{0,4},{4,8},{8,12},{12,0},{1,5},{5,9},{9,13},{13,1},{2,6},{6,10},{... | collective-permute-start | bytes 1572872 | tf_op jit(solution)/shard_map/ppermute | solution.py:17
  1437.2 23.1 %collective-permute-start.6 = (bf16[128,2048]{1,0:T(8,128)(2,1)}, bf16[128,2048]{1,0:T(8,128)(2,1)S(1)}, u32[]{:S(2)}, u32[]{:S(2)}) collective-permute-start(bf16[128,2048]{1,0:T(8,128)(2,1)} %all-reduce.2.cloned.1.call-done), channel_id=1, source_target_pairs={{0,12},{4,0},{8,4},{12,8},{1,13},{5,1},{9,5},{13,9},{2,14},{6,2},{... | collective-permute-start | bytes 1572872 | tf_op jit(solution)/shard_map/ppermute | solution.py:19
Sparse Core Ops, SparseCore 0:
  376.6 209.1 all-gather.20
  1175.0 32.3 all-gather.12
  1229.3 32.3 all-gather.14
  1283.7 32.3 all-gather.16
  1338.0 32.3 all-gather.18
  1389.8 32.7 all-reduce.1
